TPU v7x, 512 devices: a whole 4x8x8 slice. The times are simulated.
512 devices in a mesh: dp: 4 (over x), expert: 8 (over y), etp: 16 (over z, core).
Axes of the slice: x: 4, y: 8, z: 8, core: 2. Of those that a mesh axis runs over, the one named last changes fastest.
Arguments:
- tokens: bfloat16 [4096, 3072], P(('dp', 'expert')), parts along dimension 0, may hold values from -6 to 6
- routes: int32 [4096, 2], P(('dp', 'expert')), parts along dimension 0, may hold values from 0 to 3, all different within a row; in each aligned block of 128 rows (0 to 127, 128 to 255, ...) at most 80 rows name the same one
- route_weight: float32 [4096, 2], P(('dp', 'expert')), parts along dimension 0, may hold values from 0.2 to 1
- w_in: bfloat16 [8, 3072, 4096], P('expert', None, 'etp'), may hold values from -0.109375 to 0.109375
- w_out: bfloat16 [8, 4096, 3072], P('expert', 'etp'), may hold values from -0.0625 to 0.0625
Outputs:
- moe_output: bfloat16 [4096, 3072], P(('dp', 'expert')), parts along dimension 0
There are 4 independent parts, one for each index of `dp`. A program takes and returns all parts, laid end to end along the dimension named above; an argument that names none is the same for every part. Nothing has to cross between parts.
Inputs may be any that keep to these rules, and one draw needn't show every extreme that they name: `routes`: each row names two different experts. Within each aligned block of 128 rows (the rows of one index of the expert axis) no expert is named by more than 80 rows, a bound that some block reaches.
All inputs are finite; a program needn't handle non-finite values.
Results may differ from a plain program's by a relative error of at most 0.018.
Values may be sent and summed in bfloat16 or wider, within the bound.
No kernel may reach another device: no remote copies, remote signals or barrier semaphores. Data moves between devices by JAX's collectives and lax.ppermute only.
A program may use at most 64 MiB of HBM per device.

v0:
```python
import jax
import jax.numpy as jnp
from jax import lax
from jax.sharding import PartitionSpec as P


def on_device(tokens, routes, route_weight, w_in, w_out):
    n_index = lax.axis_size("expert")
    n_tensor = lax.axis_size("etp")
    halves = max(1, n_index // 4)
    n_experts = n_index // halves
    tok_rows = tokens.shape[0]
    model_width = tokens.shape[1]
    rounded_up = (2 * tok_rows // n_experts + tok_rows // 8 + n_tensor - 1) // n_tensor * n_tensor
    capacity = min(tok_rows, rounded_up)
    chosen = routes.reshape(-1)
    indicator = (chosen[:, None] == jnp.arange(n_experts, dtype=jnp.int32)[None, :]).astype(
        jnp.int32
    )
    preceding = jnp.cumsum(indicator, axis=0) - indicator
    position = jnp.sum(preceding * indicator, axis=1)
    destination = chosen * capacity + position
    duplicated = jnp.repeat(tokens, 2, axis=0)
    packed = (
        jnp.zeros((n_experts * capacity, model_width), jnp.bfloat16).at[destination].set(duplicated)
    )
    outgoing = jnp.repeat(packed.reshape(n_experts, capacity, model_width), halves, axis=0)
    w_first = w_in[0]
    w_second = w_out[0]
    arrived = lax.all_to_all(outgoing, "expert", split_axis=0, concat_axis=0, tiled=True)
    flat_rows = arrived.reshape(-1, model_width)
    projected = jnp.dot(flat_rows, w_first, preferred_element_type=jnp.float32)
    hidden = jax.nn.silu(projected).astype(jnp.bfloat16)
    term = jnp.dot(hidden, w_second, preferred_element_type=jnp.float32)
    rounded = lax.optimization_barrier(term.astype(jnp.bfloat16))
    partial_terms = rounded.astype(jnp.float32).reshape(arrived.shape[:-1] + (model_width,))
    summed = lax.psum_scatter(
        partial_terms.astype(jnp.bfloat16), "etp", scatter_dimension=1, tiled=True
    ).astype(jnp.float32)
    homeward = lax.all_to_all(
        summed.astype(jnp.bfloat16), "expert", split_axis=0, concat_axis=0, tiled=True
    ).astype(summed.dtype)
    gathered = lax.all_gather(homeward.astype(jnp.bfloat16), "etp", axis=1, tiled=True).astype(
        homeward.dtype
    )
    home_rows = gathered.reshape(n_index * capacity, model_width)
    combined = jnp.zeros((tok_rows * 2, model_width), jnp.float32)
    for half_index in range(halves):
        combined = combined + home_rows[(chosen * halves + half_index) * capacity + position]
    weighted = combined.reshape(tok_rows, 2, model_width) * route_weight[:, :, None]
    return jnp.sum(weighted, axis=1).astype(jnp.bfloat16)


def solution(mesh):
    placed = (
        P(("dp", "expert"), None),
        P(("dp", "expert"), None),
        P(("dp", "expert"), None),
        P("expert", None, "etp"),
        P("expert", "etp", None),
    )
    return jax.shard_map(
        on_device, mesh=mesh, in_specs=placed, out_specs=P(("dp", "expert"), None), check_vma=False
    )
```

profile of v0, /device:TPU:1, one launch (start us, length us, event | category | flops | bytes accessed | tf_op | source)
XLA Modules:
  0.0 307.0 jit_solution(10249326293521199883)
XLA Ops:
  6.5 0.9 copy.28
  7.4 0.1 eq.29
  7.6 0.1 eq.25
  7.7 0.7 add_multiply_fusion
  8.4 1.2 reduce-window.6
  9.7 0.1 copy.30
  9.9 0.1 copy.31
  10.0 0.1 copy.27
  10.1 0.1 mul.69
  10.3 0.1 copy.36
  10.4 0.1 mul.74
  10.5 0.1 copy.37
  10.7 0.1 mul.77
  10.8 1.9 broadcast_in_dim.7
  12.8 1.5 reshape.166
  14.3 4.2 %scatter_custom_fusion = bf16[320,3072]{1,0:T(8,128)(2,1)S(1)} fusion(s32[256]{0:T(256)S(1)} %bitcast.49, bf16[256,3072]{1,0:T(8,128)(2,1)} %reshape.166, bf16[]{:T(256)} %constant.5.clone.1), kind=kCustom, calls=%fused_computation.8 | custom fusion | bytes 1966592 | tf_op jit(solution)/shard_map/scatter | solution.py:25
  18.5 0.6 broadcast_in_dim.16
  19.1 95.2 %all_to_all.10 = bf16[8,80,3072]{2,1,0:T(8,128)(2,1)} all-to-all(bf16[8,80,3072]{2,1,0:T(8,128)(2,1)S(1)} %bitcast.41), channel_id=1, replica_groups=mesh['dp'=4,'expert'=8,'etp'=16] {'expert'}, dimensions={0} | all-to-all | bytes 7864320 | tf_op jit(solution)/shard_map/all_to_all | solution.py:30
  114.4 8.2 %convolution_convert_fusion = bf16[640,3072]{1,0:T(8,128)(2,1)} fusion(bf16[1,256,3072]{2,1,0:T(8,128)(2,1)S(1)} %copy-done, bf16[640,3072]{1,0:T(8,128)(2,1)} %bitcast.43, bf16[1,3072,256]{2,1,0:T(8,128)(2,1)S(1)} %copy-done.2), kind=kOutput, calls=%fused_computation.3 | convolution fusion | flops 2016051200 | bytes 11010048 | tf_op jit(solution)/shard_map/dot_general | solution.py:34
  122.5 6.2 %copy.32 = bf16[8,80,3072]{2,0,1:T(8,128)(2,1)} copy(bf16[8,80,3072]{2,1,0:T(8,128)(2,1)} %bitcast.44) | data formatting | bytes 7864320 | tf_op jit(solution)/shard_map/convert_element_type | solution.py:38
  128.8 66.1 %reduce-scatter.2.cloned.1.call-done = bf16[8,5,3072]{2,0,1:T(8,128)(2,1)} async-done(((bf16[8,80,3072]{2,0,1:T(8,128)(2,1)}), bf16[8,5,3072]{2,0,1:T(8,128)(2,1)}) %reduce-scatter.2.cloned.1.call-update) | async-done | bytes 245776 | tf_op jit(solution)/shard_map/reduce_scatter | solution.py:37
  194.9 1.1 copy.33
  196.0 16.7 %all_to_all.11 = bf16[8,5,3072]{2,1,0:T(8,128)(2,1)S(1)} all-to-all(bf16[8,5,3072]{2,1,0:T(8,128)(2,1)S(1)} %copy.33), channel_id=1, replica_groups=mesh['dp'=4,'expert'=8,'etp'=16] {'expert'}, dimensions={0} | all-to-all | bytes 491520 | tf_op jit(solution)/shard_map/all_to_all | solution.py:40
  212.8 0.9 copy.34
  213.7 0.1 copy.38
  213.8 45.4 %all-gather.2.cloned.1.call-done = bf16[8,80,3072]{2,0,1:T(8,128)(2,1)} async-done(((bf16[8,5,3072]{2,0,1:T(8,128)(2,1)}), bf16[8,80,3072]{2,0,1:T(8,128)(2,1)}) %all-gather.2.cloned.1.call-update) | async-done | bytes 3932176 | tf_op jit(solution)/shard_map/all_gather | solution.py:43
  259.2 7.5 %copy.35 = f32[8,80,3072]{2,1,0:T(8,128)} copy(bf16[8,80,3072]{2,0,1:T(8,128)(2,1)} %all-gather.2.cloned.1.call-done) | data formatting | bytes 11796480 | tf_op jit(solution)/shard_map/reshape | solution.py:46
  266.7 8.0 %gather_fusion.1 = f32[256,3072]{1,0:T(8,128)} fusion(f32[640,3072]{1,0:T(8,128)} %bitcast.39, s32[1024]{0:T(1024)S(1)} %pad_clamp_fusion), kind=kCustom, calls=%fused_computation.1 | custom fusion | bytes 6292480 | tf_op jit(solution)/shard_map/gather | solution.py:49
  274.7 8.0 %gather_fusion = f32[256,3072]{1,0:T(8,128)} fusion(f32[640,3072]{1,0:T(8,128)} %bitcast.40, s32[1024]{0:T(1024)S(1)} %pad_clamp_fusion.1), kind=kCustom, calls=%fused_computation | custom fusion | bytes 6292480 | tf_op jit(solution)/shard_map/gather | solution.py:49
  282.7 5.1 %add.100 = f32[256,3072]{1,0:T(8,128)} add(f32[256,3072]{1,0:T(8,128)} %gather_fusion, f32[256,3072]{1,0:T(8,128)} %gather_fusion.1) | non-fusion elementwise | flops 786432 | bytes 9437184 | tf_op jit(solution)/shard_map/add | solution.py:49
  287.8 5.1 %add.101 = f32[128,2,3072]{2,1,0:T(2,128)} reshape(f32[256,3072]{1,0:T(8,128)} %add.100) | data formatting | bytes 6291456 | tf_op jit(solution)/shard_map/add | solution.py:49
  292.8 7.3 %multiply_reduce_fusion = bf16[128,3072]{1,0:T(8,128)(2,1)} fusion(f32[128,2,3072]{2,1,0:T(2,128)} %add.101, f32[128,2]{1,0:T(8,128)S(1)} %copy.38), kind=kLoop, calls=%fused_computation.4 | loop fusion | flops 1179648 | bytes 3933184 | tf_op jit(solution)/shard_map/reduce_sum | solution.py:51
  (19 shorter events, 0.3 us)
Async XLA Ops:
  6.5 107.8 %copy-start = (bf16[1,256,3072]{2,1,0:T(8,128)(2,1)S(1)}, bf16[1,256,3072]{2,1,0:T(8,128)(2,1)}, u32[]{:S(2)}) copy-start(bf16[1,256,3072]{2,1,0:T(8,128)(2,1)} %param.9) | copy-start | bytes 4718596
  6.5 188.4 %reduce-scatter.2.cloned.1.call-start = ((), (), s32[]{:S(2)}) async-start(), calls=%async_computation.3 | async-start | bytes 4177920 | tf_op jit(solution)/shard_map/reduce_scatter | solution.py:37
  19.1 95.2 %copy-start.2 = (bf16[1,3072,256]{2,1,0:T(8,128)(2,1)S(1)}, bf16[1,3072,256]{2,1,0:T(8,128)(2,1)}, u32[]{:S(2)}) copy-start(bf16[1,3072,256]{2,1,0:T(8,128)(2,1)} %param.8) | copy-start | bytes 4718596
  128.7 84.9 %copy-start.1 = (f32[128,2]{0,1:T(2,128)S(1)}, f32[128,2]{0,1:T(2,128)}, u32[]{:S(2)}) copy-start(f32[128,2]{0,1:T(2,128)} %param.7) | copy-start | bytes 3076
  128.7 130.5 %all-gather.2.cloned.1.call-start = ((), (), s32[]{:S(2)}) async-start(), calls=%async_computation.4 | async-start | bytes 4177920 | tf_op jit(solution)/shard_map/all_gather | solution.py:43
Sparse Core Ops, SparseCore 0:
  128.9 66.0 reduce-scatter.1
  213.8 45.4 all-gather.1
where the time goes:
time: 308 us; the launch traced here: 307 us
  blocking collectives  112 us (36%)
  waiting for transfers between devices  112 us (36%)
  local copies, waits for them, and re-layouts  47.3 us (15%)
  other arithmetic  14.4 us (5%)
  between operations  13.5 us (4%)
  matrix products  8.18 us (3%)
    all_to_all x1, blocking collectives, on_device(): lax.all_to_all(outgoing, 'expert', split_axis=0, concat_axis=0, tiled=True)  95.2 us
    reduce_scatter x1, waiting for transfers between devices, on_device(): lax.psum_scatter(partial_terms.astype(jnp.bfloat16), 'etp', scatter_dimen...  66.1 us
    all_gather x1, waiting for transfers between devices, on_device(): lax.all_gather(homeward.astype(jnp.bfloat16), 'etp', axis=1, tiled=True)  45.4 us
    all_to_all x1, blocking collectives, on_device(): lax.all_to_all(summed.astype(jnp.bfloat16), 'expert', split_axis=0, conca...  16.7 us
    gather x2, local copies, waits for them, and re-layouts, on_device(): home_rows[(chosen * halves + half_index) * capacity + position]  16 us
    dot_general x1, matrix products, on_device(): term = jnp.dot(hidden, w_second, preferred_element_type=jnp.float32)  8.18 us
    reshape x1, local copies, waits for them, and re-layouts, on_device(): home_rows = gathered.reshape(n_index * capacity, model_width)  7.47 us
    reduce_sum x1, other arithmetic, on_device(): return jnp.sum(weighted, axis=1).astype(jnp.bfloat16)  7.27 us
  transfers between devices with their start and end apart: 2, of which 2 were waited for; matrix products, arithmetic and copies ran while one was open for 0% of the time, Pallas kernels for 0%

commit v1 on v0

--- a/solution.py
+++ b/solution.py
@@ -2,6 +2,27 @@
 import jax.numpy as jnp
 from jax import lax
 from jax.sharding import PartitionSpec as P
+
+
+def gather_around(value, axis, dim):
+    size, here, rows = (lax.axis_size(axis), lax.axis_index(axis), value.shape[dim])
+    right = [(i, (i + 1) % size) for i in range(size)]
+    behind = [(i, (i - 1) % size) for i in range(size)]
+    result = jnp.zeros((*value.shape[:dim], size * rows, *value.shape[dim + 1 :]), value.dtype)
+    result = lax.dynamic_update_slice_in_dim(result, value, here * rows, axis=dim)
+    from_left = from_right = value
+    middle = size // 2
+    for step in range(1, middle + 1):
+        from_left = lax.ppermute(from_left, axis, right)
+        result = lax.dynamic_update_slice_in_dim(
+            result, from_left, (here - step) % size * rows, axis=dim
+        )
+        if step < size - middle:
+            from_right = lax.ppermute(from_right, axis, behind)
+            result = lax.dynamic_update_slice_in_dim(
+                result, from_right, (here + step) % size * rows, axis=dim
+            )
+    return result
 
 
 def on_device(tokens, routes, route_weight, w_in, w_out):
@@ -40,9 +61,7 @@
     homeward = lax.all_to_all(
         summed.astype(jnp.bfloat16), "expert", split_axis=0, concat_axis=0, tiled=True
     ).astype(summed.dtype)
-    gathered = lax.all_gather(homeward.astype(jnp.bfloat16), "etp", axis=1, tiled=True).astype(
-        homeward.dtype
-    )
+    gathered = gather_around(homeward.astype(jnp.bfloat16), "etp", 1).astype(homeward.dtype)
     home_rows = gathered.reshape(n_index * capacity, model_width)
     combined = jnp.zeros((tok_rows * 2, model_width), jnp.float32)
     for half_index in range(halves):

time: 308 us -> 401 us (1.30); the launches traced: 307 us -> 393 us
  local copies, waits for them, and re-layouts: 47.3 us -> 115 us
  starting transfers between devices: 0.04 us -> 39.6 us
  waiting for transfers between devices: 112 us -> 83.8 us
  other arithmetic: 14.4 us -> 20.6 us
    dynamic_update_slice x0 -> x16, local copies, waits for them, and re-layouts: none -> 72.9 us  [the longest x8 36.2 us: gather_around(): lax.dynamic_update_slice_in_dim(result, from_left, (here - step) % size *...]
    all_gather x1 -> x0, waiting for transfers between devices: 45.4 us -> none  [on_device(): lax.all_gather(homeward.astype(jnp.bfloat16), 'etp', axis=1, tiled=True)]
    ppermute x0 -> x15, starting transfers between devices: none -> 39.6 us  [the longest x7 23.6 us: gather_around(): from_right = lax.ppermute(from_right, axis, behind)]
    ppermute x0 -> x15, waiting for transfers between devices: none -> 17.5 us  [the longest x8 12.3 us: gather_around(): from_left = lax.ppermute(from_left, axis, right)]
    reshape x1 -> x0, local copies, waits for them, and re-layouts: 7.47 us -> none  [on_device(): home_rows = gathered.reshape(n_index * capacity, model_width)]
    reshape x0 -> x1, other arithmetic: none -> 6.21 us  [on_device(): home_rows = gathered.reshape(n_index * capacity, model_width)]
  transfers between devices with their start and end apart: 2 -> 16, of which waited for: 2 -> 14; matrix products, arithmetic and copies ran while one was open for 0% -> 18% of each run, Pallas kernels for 0% -> 0%
where the time goes in v1:
time: 401 us; the launch traced here: 393 us
  local copies, waits for them, and re-layouts  115 us (29%)
  blocking collectives  112 us (28%)
  waiting for transfers between devices  83.8 us (21%)
  starting transfers between devices  39.6 us (10%)
  other arithmetic  20.6 us (5%)
  between operations  13.5 us (3%)
  matrix products  8.16 us (2%)
    all_to_all x1, blocking collectives, on_device(): lax.all_to_all(outgoing, 'expert', split_axis=0, concat_axis=0, tiled=True)  95.2 us
    reduce_scatter x1, waiting for transfers between devices, on_device(): lax.psum_scatter(partial_terms.astype(jnp.bfloat16), 'etp', scatter_dimen...  66.2 us
    dynamic_update_slice x8, local copies, waits for them, and re-layouts, gather_around(): lax.dynamic_update_slice_in_dim(result, from_left, (here - step) % size *...  36.2 us
    dynamic_update_slice x7, local copies, waits for them, and re-layouts, gather_around(): lax.dynamic_update_slice_in_dim(result, from_right, (here + step) % size...  32.3 us
    ppermute x7, starting transfers between devices, gather_around(): from_right = lax.ppermute(from_right, axis, behind)  23.6 us
    all_to_all x1, blocking collectives, on_device(): lax.all_to_all(summed.astype(jnp.bfloat16), 'expert', split_axis=0, conca...  16.7 us
    gather x2, local copies, waits for them, and re-layouts, on_device(): home_rows[(chosen * halves + half_index) * capacity + position]  16 us
    ppermute x8, starting transfers between devices, gather_around(): from_left = lax.ppermute(from_left, axis, right)  16 us
  transfers between devices with their start and end apart: 16, of which 14 were waited for; matrix products, arithmetic and copies ran while one was open for 18% of the time, Pallas kernels for 0%

profile of v1, /device:TPU:1, one launch (start us, length us, event | category | flops | bytes accessed | tf_op | source)
XLA Modules:
  0.0 392.6 jit_solution(379634610022546857)
XLA Ops:
  14.3 4.2 %scatter_custom_fusion = bf16[320,3072]{1,0:T(8,128)(2,1)S(1)} fusion(s32[256]{0:T(256)S(1)} %bitcast.49, bf16[256,3072]{1,0:T(8,128)(2,1)} %reshape.166, bf16[]{:T(256)} %constant.103.clone.1), kind=kCustom, calls=%fused_computation.9 | custom fusion | bytes 1966592 | tf_op jit(solution)/shard_map/scatter | solution.py:46
  19.2 95.2 %all_to_all.10 = bf16[8,80,3072]{2,1,0:T(8,128)(2,1)} all-to-all(bf16[8,80,3072]{2,1,0:T(8,128)(2,1)S(1)} %bitcast.41), channel_id=1, replica_groups=mesh['dp'=4,'expert'=8,'etp'=16] {'expert'}, dimensions={0} | all-to-all | bytes 7864320 | tf_op jit(solution)/shard_map/all_to_all | solution.py:51
  114.4 8.2 %convolution_convert_fusion = bf16[640,3072]{1,0:T(8,128)(2,1)} fusion(bf16[1,256,3072]{2,1,0:T(8,128)(2,1)S(1)} %copy-done, bf16[640,3072]{1,0:T(8,128)(2,1)} %bitcast.43, bf16[1,3072,256]{2,1,0:T(8,128)(2,1)S(1)} %copy-done.17), kind=kOutput, calls=%fused_computation.3 | convolution fusion | flops 2016051200 | bytes 11010048 | tf_op jit(solution)/shard_map/dot_general | solution.py:55
  122.5 6.1 %copy.47 = bf16[8,80,3072]{2,0,1:T(8,128)(2,1)} copy(bf16[8,80,3072]{2,1,0:T(8,128)(2,1)} %bitcast.44) | data formatting | bytes 7864320 | tf_op jit(solution)/shard_map/convert_element_type | solution.py:59
  128.7 66.2 %reduce-scatter.2.cloned.1.call-done = bf16[8,5,3072]{2,0,1:T(8,128)(2,1)} async-done(((bf16[8,80,3072]{2,0,1:T(8,128)(2,1)}), bf16[8,5,3072]{2,0,1:T(8,128)(2,1)}) %reduce-scatter.2.cloned.1.call-update) | async-done | bytes 245776 | tf_op jit(solution)/shard_map/reduce_scatter | solution.py:58
  196.0 16.7 %all_to_all.11 = bf16[8,5,3072]{2,1,0:T(8,128)(2,1)S(1)} all-to-all(bf16[8,5,3072]{2,1,0:T(8,128)(2,1)S(1)} %copy.48), channel_id=1, replica_groups=mesh['dp'=4,'expert'=8,'etp'=16] {'expert'}, dimensions={0} | all-to-all | bytes 491520 | tf_op jit(solution)/shard_map/all_to_all | solution.py:61
  212.7 5.2 %collective-permute-start = (bf16[8,5,3072]{2,1,0:T(8,128)(2,1)S(1)}, bf16[8,5,3072]{2,1,0:T(8,128)(2,1)S(1)}, u32[]{:S(2)}, u32[]{:S(2)}) collective-permute-start(bf16[8,5,3072]{2,1,0:T(8,128)(2,1)S(1)} %all_to_all.11), channel_id=1, source_target_pairs={{0,1},{1,2},{2,3},{3,4},{4,5},{5,6},{6,7},{7,8},{8,9},{9,10},{10,1... | collective-permute-start | bytes 737288 | tf_op jit(solution)/shard_map/ppermute | solution.py:16
  217.9 4.7 %collective-permute-done = bf16[8,5,3072]{2,1,0:T(8,128)(2,1)S(1)} collective-permute-done((bf16[8,5,3072]{2,1,0:T(8,128)(2,1)S(1)}, bf16[8,5,3072]{2,1,0:T(8,128)(2,1)S(1)}, u32[]{:S(2)}, u32[]{:S(2)}) %collective-permute-start) | collective-permute-done | bytes 245792 | tf_op jit(solution)/shard_map/ppermute | solution.py:16
  247.9 4.5 %collective-permute-start.9 = (bf16[8,5,3072]{2,1,0:T(8,128)(2,1)S(1)}, bf16[8,5,3072]{2,1,0:T(8,128)(2,1)S(1)}, u32[]{:S(2)}, u32[]{:S(2)}) collective-permute-start(bf16[8,5,3072]{2,1,0:T(8,128)(2,1)S(1)} %collective-permute-done.7), channel_id=1, source_target_pairs={{0,15},{1,0},{2,1},{3,2},{4,3},{5,4},{6,5},{7,6},{8,7},{9,8},{10,9... | collective-permute-start | bytes 737288 | tf_op jit(solution)/shard_map/ppermute | solution.py:21
  255.2 5.7 %collective-permute-start.11 = (bf16[8,5,3072]{2,1,0:T(8,128)(2,1)S(1)}, bf16[8,5,3072]{2,1,0:T(8,128)(2,1)}, u32[]{:S(2)}, u32[]{:S(2)}) collective-permute-start(bf16[8,5,3072]{2,1,0:T(8,128)(2,1)S(1)} %collective-permute-done.9), channel_id=1, source_target_pairs={{0,15},{1,0},{2,1},{3,2},{4,3},{5,4},{6,5},{7,6},{8,7},{9,8},{10,9... | collective-permute-start | bytes 737288 | tf_op jit(solution)/shard_map/ppermute | solution.py:21
  262.5 6.8 %collective-permute-start.13 = (bf16[8,5,3072]{2,1,0:T(8,128)(2,1)}, bf16[8,5,3072]{2,1,0:T(8,128)(2,1)}, u32[]{:S(2)}, u32[]{:S(2)}) collective-permute-start(bf16[8,5,3072]{2,1,0:T(8,128)(2,1)} %collective-permute-done.11), channel_id=1, source_target_pairs={{0,15},{1,0},{2,1},{3,2},{4,3},{5,4},{6,5},{7,6},{8,7},{9,8},{10,9... | collective-permute-start | bytes 737288 | tf_op jit(solution)/shard_map/ppermute | solution.py:21
  273.1 4.5 %dynamic_update_slice.48 = bf16[8,80,3072]{2,1,0:T(8,128)(2,1)} dynamic-update-slice(bf16[8,80,3072]{2,1,0:T(8,128)(2,1)} %broadcast_in_dim.8, bf16[8,5,3072]{2,1,0:T(8,128)(2,1)S(1)} %all_to_all.11, s32[]{:T(128)} %constant.105.clone.1, s32[]{:T(128)S(6)} %select_n.142, s32[]{:T(128)} %constant.105.clone.1) | dynamic-update-slice | bytes 491524 | tf_op jit(solution)/shard_map/dynamic_update_slice | solution.py:12
  277.6 4.5 %dynamic_update_slice.49 = bf16[8,80,3072]{2,1,0:T(8,128)(2,1)} dynamic-update-slice(bf16[8,80,3072]{2,1,0:T(8,128)(2,1)} %dynamic_update_slice.48, bf16[8,5,3072]{2,1,0:T(8,128)(2,1)S(1)} %collective-permute-done, s32[]{:T(128)} %constant.105.clone.1, s32[]{:T(128)S(6)} %select_n.144, s32[]{:T(128)} %constant.105.clone.1) | dynamic-update-slice | bytes 491524 | tf_op jit(solution)/shard_map/dynamic_update_slice | solution.py:17
  282.1 4.6 %dynamic_update_slice.50 = bf16[8,80,3072]{2,1,0:T(8,128)(2,1)} dynamic-update-slice(bf16[8,80,3072]{2,1,0:T(8,128)(2,1)} %dynamic_update_slice.49, bf16[8,5,3072]{2,1,0:T(8,128)(2,1)S(1)} %collective-permute-done.1, s32[]{:T(128)} %constant.105.clone.1, s32[]{:T(128)S(6)} %select_n.146, s32[]{:T(128)} %constant.105.clone.1) | dynamic-update-slice | bytes 491524 | tf_op jit(solution)/shard_map/dynamic_update_slice | solution.py:22
  290.6 4.6 %dynamic_update_slice.52 = bf16[8,80,3072]{2,1,0:T(8,128)(2,1)} dynamic-update-slice(bf16[8,80,3072]{2,1,0:T(8,128)(2,1)} %dynamic_update_slice.51, bf16[8,5,3072]{2,1,0:T(8,128)(2,1)S(1)} %collective-permute-done.3, s32[]{:T(128)} %constant.105.clone.1, s32[]{:T(128)S(6)} %select_n.150, s32[]{:T(128)} %constant.105.clone.1) | dynamic-update-slice | bytes 491524 | tf_op jit(solution)/shard_map/dynamic_update_slice | solution.py:22
  295.2 4.6 %dynamic_update_slice.53 = bf16[8,80,3072]{2,1,0:T(8,128)(2,1)} dynamic-update-slice(bf16[8,80,3072]{2,1,0:T(8,128)(2,1)} %dynamic_update_slice.52, bf16[8,5,3072]{2,1,0:T(8,128)(2,1)S(1)} %copy-done.2, s32[]{:T(128)} %constant.105.clone.1, s32[]{:T(128)S(6)} %select_n.152, s32[]{:T(128)} %constant.105.clone.1) | dynamic-update-slice | bytes 491524 | tf_op jit(solution)/shard_map/dynamic_update_slice | solution.py:17
  299.8 4.6 %dynamic_update_slice.54 = bf16[8,80,3072]{2,1,0:T(8,128)(2,1)} dynamic-update-slice(bf16[8,80,3072]{2,1,0:T(8,128)(2,1)} %dynamic_update_slice.53, bf16[8,5,3072]{2,1,0:T(8,128)(2,1)S(1)} %copy-done.4, s32[]{:T(128)} %constant.105.clone.1, s32[]{:T(128)S(6)} %select_n.154, s32[]{:T(128)} %constant.105.clone.1) | dynamic-update-slice | bytes 491524 | tf_op jit(solution)/shard_map/dynamic_update_slice | solution.py:22
  304.4 4.6 %dynamic_update_slice.55 = bf16[8,80,3072]{2,1,0:T(8,128)(2,1)} dynamic-update-slice(bf16[8,80,3072]{2,1,0:T(8,128)(2,1)} %dynamic_update_slice.54, bf16[8,5,3072]{2,1,0:T(8,128)(2,1)S(1)} %copy-done.6, s32[]{:T(128)} %constant.105.clone.1, s32[]{:T(128)S(6)} %select_n.156, s32[]{:T(128)} %constant.105.clone.1) | dynamic-update-slice | bytes 491524 | tf_op jit(solution)/shard_map/dynamic_update_slice | solution.py:17
  308.9 4.5 %dynamic_update_slice.56 = bf16[8,80,3072]{2,1,0:T(8,128)(2,1)} dynamic-update-slice(bf16[8,80,3072]{2,1,0:T(8,128)(2,1)} %dynamic_update_slice.55, bf16[8,5,3072]{2,1,0:T(8,128)(2,1)S(1)} %copy-done.8, s32[]{:T(128)} %constant.105.clone.1, s32[]{:T(128)S(6)} %select_n.158, s32[]{:T(128)} %constant.105.clone.1) | dynamic-update-slice | bytes 491524 | tf_op jit(solution)/shard_map/dynamic_update_slice | solution.py:22
  313.4 4.5 %dynamic_update_slice.57 = bf16[8,80,3072]{2,1,0:T(8,128)(2,1)} dynamic-update-slice(bf16[8,80,3072]{2,1,0:T(8,128)(2,1)} %dynamic_update_slice.56, bf16[8,5,3072]{2,1,0:T(8,128)(2,1)S(1)} %copy-done.10, s32[]{:T(128)} %constant.105.clone.1, s32[]{:T(128)S(6)} %select_n.160, s32[]{:T(128)} %constant.105.clone.1) | dynamic-update-slice | bytes 491524 | tf_op jit(solution)/shard_map/dynamic_update_slice | solution.py:17
  318.0 4.5 %dynamic_update_slice.58 = bf16[8,80,3072]{2,1,0:T(8,128)(2,1)} dynamic-update-slice(bf16[8,80,3072]{2,1,0:T(8,128)(2,1)} %dynamic_update_slice.57, bf16[8,5,3072]{2,1,0:T(8,128)(2,1)S(1)} %copy-done.12, s32[]{:T(128)} %constant.105.clone.1, s32[]{:T(128)S(6)} %select_n.162, s32[]{:T(128)} %constant.105.clone.1) | dynamic-update-slice | bytes 491524 | tf_op jit(solution)/shard_map/dynamic_update_slice | solution.py:22
  322.5 4.5 %dynamic_update_slice.59 = bf16[8,80,3072]{2,1,0:T(8,128)(2,1)} dynamic-update-slice(bf16[8,80,3072]{2,1,0:T(8,128)(2,1)} %dynamic_update_slice.58, bf16[8,5,3072]{2,1,0:T(8,128)(2,1)S(1)} %copy-done.14, s32[]{:T(128)} %constant.105.clone.1, s32[]{:T(128)S(6)} %select_n.164, s32[]{:T(128)} %constant.105.clone.1) | dynamic-update-slice | bytes 491524 | tf_op jit(solution)/shard_map/dynamic_update_slice | solution.py:17
  327.0 4.7 %dynamic_update_slice.60 = bf16[8,80,3072]{2,1,0:T(8,128)(2,1)} dynamic-update-slice(bf16[8,80,3072]{2,1,0:T(8,128)(2,1)} %dynamic_update_slice.59, bf16[8,5,3072]{2,1,0:T(8,128)(2,1)} %collective-permute-done.11, s32[]{:T(128)} %constant.105.clone.1, s32[]{:T(128)S(6)} %select_n.166, s32[]{:T(128)} %constant.105.clone.1) | dynamic-update-slice | bytes 491524 | tf_op jit(solution)/shard_map/dynamic_update_slice | solution.py:22
  331.8 4.7 %dynamic_update_slice.61 = bf16[8,80,3072]{2,1,0:T(8,128)(2,1)} dynamic-update-slice(bf16[8,80,3072]{2,1,0:T(8,128)(2,1)} %dynamic_update_slice.60, bf16[8,5,3072]{2,1,0:T(8,128)(2,1)} %collective-permute-done.12, s32[]{:T(128)} %constant.105.clone.1, s32[]{:T(128)S(6)} %select_n.168, s32[]{:T(128)} %constant.105.clone.1) | dynamic-update-slice | bytes 491524 | tf_op jit(solution)/shard_map/dynamic_update_slice | solution.py:17
  336.5 4.8 %dynamic_update_slice.62 = bf16[8,80,3072]{2,1,0:T(8,128)(2,1)} dynamic-update-slice(bf16[8,80,3072]{2,1,0:T(8,128)(2,1)} %dynamic_update_slice.61, bf16[8,5,3072]{2,1,0:T(8,128)(2,1)} %collective-permute-done.13, s32[]{:T(128)} %constant.105.clone.1, s32[]{:T(128)S(6)} %select_n.170, s32[]{:T(128)} %constant.105.clone.1) | dynamic-update-slice | bytes 491524 | tf_op jit(solution)/shard_map/dynamic_update_slice | solution.py:22
  341.3 4.8 %dynamic_update_slice.63 = bf16[8,80,3072]{2,1,0:T(8,128)(2,1)} dynamic-update-slice(bf16[8,80,3072]{2,1,0:T(8,128)(2,1)} %dynamic_update_slice.62, bf16[8,5,3072]{2,1,0:T(8,128)(2,1)} %collective-permute-done.14, s32[]{:T(128)} %constant.105.clone.1, s32[]{:T(128)S(6)} %select_n.172, s32[]{:T(128)} %constant.105.clone.1) | dynamic-update-slice | bytes 491524 | tf_op jit(solution)/shard_map/dynamic_update_slice | solution.py:17
  346.1 6.2 %bitcast_convert_fusion = f32[640,3072]{1,0:T(8,128)} fusion(bf16[8,80,3072]{2,1,0:T(8,128)(2,1)} %dynamic_update_slice.63), kind=kLoop, calls=%fused_computation.4 | loop fusion | flops 1966080 | bytes 11796480 | tf_op jit(solution)/shard_map/reshape | solution.py:65
  352.3 8.0 %gather_fusion.1 = f32[256,3072]{1,0:T(8,128)} fusion(f32[640,3072]{1,0:T(8,128)} %bitcast_convert_fusion, s32[1024]{0:T(1024)S(1)} %pad_clamp_fusion), kind=kCustom, calls=%fused_computation.1 | custom fusion | bytes 6292480 | tf_op jit(solution)/shard_map/gather | solution.py:68
  360.3 8.0 %gather_fusion = f32[256,3072]{1,0:T(8,128)} fusion(f32[640,3072]{1,0:T(8,128)} %bitcast_convert_fusion, s32[1024]{0:T(1024)S(1)} %pad_clamp_fusion.1), kind=kCustom, calls=%fused_computation | custom fusion | bytes 6292480 | tf_op jit(solution)/shard_map/gather | solution.py:68
  368.3 5.1 %add.261 = f32[256,3072]{1,0:T(8,128)} add(f32[256,3072]{1,0:T(8,128)} %gather_fusion, f32[256,3072]{1,0:T(8,128)} %gather_fusion.1) | non-fusion elementwise | flops 786432 | bytes 9437184 | tf_op jit(solution)/shard_map/add | solution.py:68
  373.4 5.1 %add.262 = f32[128,2,3072]{2,1,0:T(2,128)} reshape(f32[256,3072]{1,0:T(8,128)} %add.261) | data formatting | bytes 6291456 | tf_op jit(solution)/shard_map/add | solution.py:68
  378.5 7.3 %multiply_reduce_fusion = bf16[128,3072]{1,0:T(8,128)(2,1)} fusion(f32[128,2,3072]{2,1,0:T(2,128)} %add.262, f32[128,2]{1,0:T(8,128)S(1)} %copy-done.15), kind=kLoop, calls=%fused_computation.5 | loop fusion | flops 1179648 | bytes 3933184 | tf_op jit(solution)/shard_map/reduce_sum | solution.py:70
  (92 shorter events, 46.7 us)
Async XLA Ops:
  6.5 107.8 %copy-start = (bf16[1,256,3072]{2,1,0:T(8,128)(2,1)S(1)}, bf16[1,256,3072]{2,1,0:T(8,128)(2,1)}, u32[]{:S(2)}) copy-start(bf16[1,256,3072]{2,1,0:T(8,128)(2,1)} %param.9) | copy-start | bytes 4718596
  6.5 188.4 %reduce-scatter.2.cloned.1.call-start = ((), (), s32[]{:S(2)}) async-start(), calls=%async_computation.3 | async-start | bytes 4177920 | tf_op jit(solution)/shard_map/reduce_scatter | solution.py:58
  19.1 95.2 %copy-start.17 = (bf16[1,3072,256]{2,1,0:T(8,128)(2,1)S(1)}, bf16[1,3072,256]{2,1,0:T(8,128)(2,1)}, u32[]{:S(2)}) copy-start(bf16[1,3072,256]{2,1,0:T(8,128)(2,1)} %param.8) | copy-start | bytes 4718596
  128.7 141.2 %copy-start.16 = (f32[128,2]{0,1:T(2,128)S(1)}, f32[128,2]{0,1:T(2,128)}, u32[]{:S(2)}) copy-start(f32[128,2]{0,1:T(2,128)} %param.7) | copy-start | bytes 3076
  212.7 10.0 %collective-permute-start = (bf16[8,5,3072]{2,1,0:T(8,128)(2,1)S(1)}, bf16[8,5,3072]{2,1,0:T(8,128)(2,1)S(1)}, u32[]{:S(2)}, u32[]{:S(2)}) collective-permute-start(bf16[8,5,3072]{2,1,0:T(8,128)(2,1)S(1)} %all_to_all.11), channel_id=1, source_target_pairs={{0,1},{1,2},{2,3},{3,4},{4,5},{5,6},{6,7},{7,8},{8,9},{9,10},{10,1... | collective-permute-start | bytes 737288 | tf_op jit(solution)/shard_map/ppermute | solution.py:16
  217.9 7.5 %collective-permute-start.1 = (bf16[8,5,3072]{2,1,0:T(8,128)(2,1)S(1)}, bf16[8,5,3072]{2,1,0:T(8,128)(2,1)S(1)}, u32[]{:S(2)}, u32[]{:S(2)}) collective-permute-start(bf16[8,5,3072]{2,1,0:T(8,128)(2,1)S(1)} %all_to_all.11), channel_id=1, source_target_pairs={{0,15},{1,0},{2,1},{3,2},{4,3},{5,4},{6,5},{7,6},{8,7},{9,8},{10,9... | collective-permute-start | bytes 737288 | tf_op jit(solution)/shard_map/ppermute | solution.py:21
  222.7 7.2 %collective-permute-start.2 = (bf16[8,5,3072]{2,1,0:T(8,128)(2,1)S(1)}, bf16[8,5,3072]{2,1,0:T(8,128)(2,1)S(1)}, u32[]{:S(2)}, u32[]{:S(2)}) collective-permute-start(bf16[8,5,3072]{2,1,0:T(8,128)(2,1)S(1)} %collective-permute-done), channel_id=1, source_target_pairs={{0,1},{1,2},{2,3},{3,4},{4,5},{5,6},{6,7},{7,8},{8,9},{9,10},{10,1... | collective-permute-start | bytes 737288 | tf_op jit(solution)/shard_map/ppermute | solution.py:16
  225.4 7.5 %collective-permute-start.3 = (bf16[8,5,3072]{2,1,0:T(8,128)(2,1)S(1)}, bf16[8,5,3072]{2,1,0:T(8,128)(2,1)S(1)}, u32[]{:S(2)}, u32[]{:S(2)}) collective-permute-start(bf16[8,5,3072]{2,1,0:T(8,128)(2,1)S(1)} %collective-permute-done.1), channel_id=1, source_target_pairs={{0,15},{1,0},{2,1},{3,2},{4,3},{5,4},{6,5},{7,6},{8,7},{9,8},{10,9... | collective-permute-start | bytes 737288 | tf_op jit(solution)/shard_map/ppermute | solution.py:21
  229.9 7.2 %collective-permute-start.4 = (bf16[8,5,3072]{2,1,0:T(8,128)(2,1)S(1)}, bf16[8,5,3072]{2,1,0:T(8,128)(2,1)S(1)}, u32[]{:S(2)}, u32[]{:S(2)}) collective-permute-start(bf16[8,5,3072]{2,1,0:T(8,128)(2,1)S(1)} %collective-permute-done.2), channel_id=1, source_target_pairs={{0,1},{1,2},{2,3},{3,4},{4,5},{5,6},{6,7},{7,8},{8,9},{9,10},{10,1... | collective-permute-start | bytes 737288 | tf_op jit(solution)/shard_map/ppermute | solution.py:16
  232.9 7.5 %collective-permute-start.5 = (bf16[8,5,3072]{2,1,0:T(8,128)(2,1)S(1)}, bf16[8,5,3072]{2,1,0:T(8,128)(2,1)S(1)}, u32[]{:S(2)}, u32[]{:S(2)}) collective-permute-start(bf16[8,5,3072]{2,1,0:T(8,128)(2,1)S(1)} %collective-permute-done.3), channel_id=1, source_target_pairs={{0,15},{1,0},{2,1},{3,2},{4,3},{5,4},{6,5},{7,6},{8,7},{9,8},{10,9... | collective-permute-start | bytes 737288 | tf_op jit(solution)/shard_map/ppermute | solution.py:21
  237.1 3.4 copy-start.1
  237.1 7.4 %collective-permute-start.6 = (bf16[8,5,3072]{2,1,0:T(8,128)(2,1)S(1)}, bf16[8,5,3072]{2,1,0:T(8,128)(2,1)S(1)}, u32[]{:S(2)}, u32[]{:S(2)}) collective-permute-start(bf16[8,5,3072]{2,1,0:T(8,128)(2,1)S(1)} %collective-permute-done.4), channel_id=1, source_target_pairs={{0,1},{1,2},{2,3},{3,4},{4,5},{5,6},{6,7},{7,8},{8,9},{9,10},{10,1... | collective-permute-start | bytes 737288 | tf_op jit(solution)/shard_map/ppermute | solution.py:16
  240.4 4.1 %copy-start.3 = (bf16[8,5,3072]{2,1,0:T(8,128)(2,1)}, bf16[8,5,3072]{2,1,0:T(8,128)(2,1)S(1)}, u32[]{:S(2)}) copy-start(bf16[8,5,3072]{2,1,0:T(8,128)(2,1)S(1)} %collective-permute-done.5) | copy-start | bytes 737284
  240.4 7.5 %collective-permute-start.7 = (bf16[8,5,3072]{2,1,0:T(8,128)(2,1)S(1)}, bf16[8,5,3072]{2,1,0:T(8,128)(2,1)S(1)}, u32[]{:S(2)}, u32[]{:S(2)}) collective-permute-start(bf16[8,5,3072]{2,1,0:T(8,128)(2,1)S(1)} %collective-permute-done.5), channel_id=1, source_target_pairs={{0,15},{1,0},{2,1},{3,2},{4,3},{5,4},{6,5},{7,6},{8,7},{9,8},{10,9... | collective-permute-start | bytes 737288 | tf_op jit(solution)/shard_map/ppermute | solution.py:21
  244.5 3.4 copy-start.5
  244.5 8.4 %collective-permute-start.8 = (bf16[8,5,3072]{2,1,0:T(8,128)(2,1)S(1)}, bf16[8,5,3072]{2,1,0:T(8,128)(2,1)S(1)}, u32[]{:S(2)}, u32[]{:S(2)}) collective-permute-start(bf16[8,5,3072]{2,1,0:T(8,128)(2,1)S(1)} %collective-permute-done.6), channel_id=1, source_target_pairs={{0,1},{1,2},{2,3},{3,4},{4,5},{5,6},{6,7},{7,8},{8,9},{9,10},{10,1... | collective-permute-start | bytes 737288 | tf_op jit(solution)/shard_map/ppermute | solution.py:16
  247.9 5.0 %copy-start.7 = (bf16[8,5,3072]{2,1,0:T(8,128)(2,1)}, bf16[8,5,3072]{2,1,0:T(8,128)(2,1)S(1)}, u32[]{:S(2)}) copy-start(bf16[8,5,3072]{2,1,0:T(8,128)(2,1)S(1)} %collective-permute-done.7) | copy-start | bytes 737284
  247.9 7.2 %collective-permute-start.9 = (bf16[8,5,3072]{2,1,0:T(8,128)(2,1)S(1)}, bf16[8,5,3072]{2,1,0:T(8,128)(2,1)S(1)}, u32[]{:S(2)}, u32[]{:S(2)}) collective-permute-start(bf16[8,5,3072]{2,1,0:T(8,128)(2,1)S(1)} %collective-permute-done.7), channel_id=1, source_target_pairs={{0,15},{1,0},{2,1},{3,2},{4,3},{5,4},{6,5},{7,6},{8,7},{9,8},{10,9... | collective-permute-start | bytes 737288 | tf_op jit(solution)/shard_map/ppermute | solution.py:21
  252.9 8.4 %collective-permute-start.10 = (bf16[8,5,3072]{2,1,0:T(8,128)(2,1)S(1)}, bf16[8,5,3072]{2,1,0:T(8,128)(2,1)S(1)}, u32[]{:S(2)}, u32[]{:S(2)}) collective-permute-start(bf16[8,5,3072]{2,1,0:T(8,128)(2,1)S(1)} %collective-permute-done.8), channel_id=1, source_target_pairs={{0,1},{1,2},{2,3},{3,4},{4,5},{5,6},{6,7},{7,8},{8,9},{9,10},{10,1... | collective-permute-start | bytes 737288 | tf_op jit(solution)/shard_map/ppermute | solution.py:16
  255.1 6.2 %copy-start.11 = (bf16[8,5,3072]{2,1,0:T(8,128)(2,1)}, bf16[8,5,3072]{2,1,0:T(8,128)(2,1)S(1)}, u32[]{:S(2)}) copy-start(bf16[8,5,3072]{2,1,0:T(8,128)(2,1)S(1)} %collective-permute-done.9) | copy-start | bytes 737284
  255.2 7.3 %collective-permute-start.11 = (bf16[8,5,3072]{2,1,0:T(8,128)(2,1)S(1)}, bf16[8,5,3072]{2,1,0:T(8,128)(2,1)}, u32[]{:S(2)}, u32[]{:S(2)}) collective-permute-start(bf16[8,5,3072]{2,1,0:T(8,128)(2,1)S(1)} %collective-permute-done.9), channel_id=1, source_target_pairs={{0,15},{1,0},{2,1},{3,2},{4,3},{5,4},{6,5},{7,6},{8,7},{9,8},{10,9... | collective-permute-start | bytes 737288 | tf_op jit(solution)/shard_map/ppermute | solution.py:21
  261.3 8.5 %collective-permute-start.12 = (bf16[8,5,3072]{2,1,0:T(8,128)(2,1)S(1)}, bf16[8,5,3072]{2,1,0:T(8,128)(2,1)}, u32[]{:S(2)}, u32[]{:S(2)}) collective-permute-start(bf16[8,5,3072]{2,1,0:T(8,128)(2,1)S(1)} %collective-permute-done.10), channel_id=1, source_target_pairs={{0,1},{1,2},{2,3},{3,4},{4,5},{5,6},{6,7},{7,8},{8,9},{9,10},{10,1... | collective-permute-start | bytes 737288 | tf_op jit(solution)/shard_map/ppermute | solution.py:16
  262.5 74.1 %collective-permute-start.13 = (bf16[8,5,3072]{2,1,0:T(8,128)(2,1)}, bf16[8,5,3072]{2,1,0:T(8,128)(2,1)}, u32[]{:S(2)}, u32[]{:S(2)}) collective-permute-start(bf16[8,5,3072]{2,1,0:T(8,128)(2,1)} %collective-permute-done.11), channel_id=1, source_target_pairs={{0,15},{1,0},{2,1},{3,2},{4,3},{5,4},{6,5},{7,6},{8,7},{9,8},{10,9... | collective-permute-start | bytes 737288 | tf_op jit(solution)/shard_map/ppermute | solution.py:21
  269.9 71.4 %collective-permute-start.14 = (bf16[8,5,3072]{2,1,0:T(8,128)(2,1)}, bf16[8,5,3072]{2,1,0:T(8,128)(2,1)}, u32[]{:S(2)}, u32[]{:S(2)}) collective-permute-start(bf16[8,5,3072]{2,1,0:T(8,128)(2,1)} %collective-permute-done.12), channel_id=1, source_target_pairs={{0,1},{1,2},{2,3},{3,4},{4,5},{5,6},{6,7},{7,8},{8,9},{9,10},{10,1... | collective-permute-start | bytes 737288 | tf_op jit(solution)/shard_map/ppermute | solution.py:16
  277.6 17.6 %copy-start.2 = (bf16[8,5,3072]{2,1,0:T(8,128)(2,1)S(1)}, bf16[8,5,3072]{2,1,0:T(8,128)(2,1)}, u32[]{:S(2)}) copy-start(bf16[8,5,3072]{2,1,0:T(8,128)(2,1)} %copy-done.1) | copy-start | bytes 737284
  282.1 17.7 %copy-start.4 = (bf16[8,5,3072]{2,1,0:T(8,128)(2,1)S(1)}, bf16[8,5,3072]{2,1,0:T(8,128)(2,1)}, u32[]{:S(2)}) copy-start(bf16[8,5,3072]{2,1,0:T(8,128)(2,1)} %copy-done.3) | copy-start | bytes 737284
  286.7 17.7 %copy-start.6 = (bf16[8,5,3072]{2,1,0:T(8,128)(2,1)S(1)}, bf16[8,5,3072]{2,1,0:T(8,128)(2,1)}, u32[]{:S(2)}) copy-start(bf16[8,5,3072]{2,1,0:T(8,128)(2,1)} %copy-done.5) | copy-start | bytes 737284
  290.6 18.3 %copy-start.8 = (bf16[8,5,3072]{2,1,0:T(8,128)(2,1)S(1)}, bf16[8,5,3072]{2,1,0:T(8,128)(2,1)}, u32[]{:S(2)}) copy-start(bf16[8,5,3072]{2,1,0:T(8,128)(2,1)} %copy-done.7) | copy-start | bytes 737284
  295.2 18.2 %copy-start.10 = (bf16[8,5,3072]{2,1,0:T(8,128)(2,1)S(1)}, bf16[8,5,3072]{2,1,0:T(8,128)(2,1)}, u32[]{:S(2)}) copy-start(bf16[8,5,3072]{2,1,0:T(8,128)(2,1)} %copy-done.9) | copy-start | bytes 737284
  299.8 18.2 %copy-start.12 = (bf16[8,5,3072]{2,1,0:T(8,128)(2,1)S(1)}, bf16[8,5,3072]{2,1,0:T(8,128)(2,1)}, u32[]{:S(2)}) copy-start(bf16[8,5,3072]{2,1,0:T(8,128)(2,1)} %copy-done.11) | copy-start | bytes 737284
  304.4 18.1 %copy-start.14 = (bf16[8,5,3072]{2,1,0:T(8,128)(2,1)S(1)}, bf16[8,5,3072]{2,1,0:T(8,128)(2,1)}, u32[]{:S(2)}) copy-start(bf16[8,5,3072]{2,1,0:T(8,128)(2,1)} %copy-done.13) | copy-start | bytes 737284
  373.4 5.1 %copy-start.15 = (f32[128,2]{1,0:T(8,128)S(1)}, f32[128,2]{1,0:T(8,128)}, u32[]{:S(2)}) copy-start(f32[128,2]{1,0:T(8,128)} %copy.51) | copy-start | bytes 3076
  (2 other events, 3.3 us)
Sparse Core Ops, SparseCore 0:
  128.8 66.0 reduce-scatter.1
